TPU v7x, 32 devices: a whole 2x2x4 slice. The times are simulated.
32 devices in a mesh: lat: 4 (over y, x), lon: 8 (over z, core).
Axes of the slice: x: 2, y: 2, z: 4, core: 2. Of those that a mesh axis runs over, the one named last changes fastest.
Arguments:
- increment: float32 [4, 20, 128, 512], P(None, None, 'lon', 'lat'), may hold values from -6 to 6
- obs_dep: float32 [4, 20, 128, 512], P(None, None, 'lon', 'lat'), may hold values from -6 to 6
- obs_weight: float32 [4, 20, 128, 512], P(None, None, 'lon', 'lat'), may hold values from 0.1 to 10
- dep_lon: int32 [20, 128, 512], P(None, 'lon', 'lat'), may hold values from -5 to 5
- dep_lat: int32 [20, 128, 512], P(None, 'lon', 'lat'), may hold values from -5 to 5
- frac_lon: float32 [20, 128, 512], P(None, 'lon', 'lat'), may hold values from 0 to 1
- frac_lat: float32 [20, 128, 512], P(None, 'lon', 'lat'), may hold values from 0 to 1
- coupling: float32 [4, 19, 128, 512], P(None, None, 'lon', 'lat'), may hold values from 0.05 to 5
Outputs:
- tl_out: float32 [4, 20, 128, 512], P(None, None, 'lon', 'lat')
- gradient: float32 [4, 20, 128, 512], P(None, None, 'lon', 'lat')
All inputs are finite; a program needn't handle non-finite values.
Results may differ from a plain program's by a relative error of at most 0.0003.
Values sent between devices are 32-bit elements; how exact they have to be, the bound alone decides.
A program may use at most 128 MiB of HBM per device.

v0:
```python
import jax
import jax.numpy as jnp
from jax import lax
from jax.sharding import PartitionSpec as P

HALO = 6


def extended_2(cells, sides, width, closed):
    for axis, dim in sides:
        count = lax.axis_size(axis)
        ends = count if closed else count - 1
        head = lax.slice_in_dim(cells, 0, width, axis=dim)
        tail = lax.slice_in_dim(cells, cells.shape[dim] - width, cells.shape[dim], axis=dim)
        cells = jnp.concatenate(
            [
                lax.ppermute(tail, axis, [(i, (i + 1) % count) for i in range(ends)]),
                cells,
                lax.ppermute(head, axis, [((i + 1) % count, i) for i in range(ends)]),
            ],
            axis=dim,
        )
    return cells


def column_solve(rhs, coup):
    levels = rhs.shape[1]
    nothing = jnp.zeros_like(rhs[:, 0])
    ratios = []
    primes = []
    for level in range(levels):
        below = coup[:, level - 1] if level > 0 else nothing
        above = coup[:, level] if level < levels - 1 else nothing
        diagonal = 1.0 + below + above
        if level == 0:
            denom = diagonal
            prime = rhs[:, 0] / denom
        else:
            denom = diagonal - below * ratios[-1]
            prime = (rhs[:, level] + below * primes[-1]) / denom
        ratios.append(above / denom)
        primes.append(prime)
    result = [primes[-1]]
    for level in range(levels - 2, -1, -1):
        result.append(primes[level] + ratios[level] * result[-1])
    ordered = result[::-1]
    return jnp.stack(ordered, axis=1)


def shift_weights(offset, frac):
    zeros = jnp.zeros_like(frac)
    listed = []
    for total in range(1 - HALO, HALO + 1):
        first = jnp.where(offset == total, 1.0 - frac, zeros)
        second = jnp.where(offset == total - 1, frac, zeros)
        listed.append(first + second)
    return listed


def interpolate(extended, olon, olat, flon, flat):
    rows, cols = (olon.shape[1], olon.shape[2])
    lon_weights = shift_weights(olon, flon)
    lat_weights = shift_weights(olat, flat)
    total = None
    for lon_pos, lon_shift in enumerate(range(1 - HALO, HALO + 1)):
        inner = None
        for lat_pos, lat_shift in enumerate(range(1 - HALO, HALO + 1)):
            piece = extended[
                :,
                :,
                HALO - lon_shift : HALO - lon_shift + rows,
                HALO - lat_shift : HALO - lat_shift + cols,
            ]
            term = lat_weights[lat_pos][None] * piece
            inner = term if inner is None else inner + term
        term = lon_weights[lon_pos][None] * inner
        total = term if total is None else total + term
    return total


def collect_own(wide_values, olon, olat, flon, flat, rows, cols):
    lon_weights = shift_weights(olon, flon)
    lat_weights = shift_weights(olat, flat)
    total = None
    for lon_pos, lon_shift in enumerate(range(1 - HALO, HALO + 1)):
        start_lon = HALO + lon_shift
        scaled = (
            lon_weights[lon_pos][None, :, start_lon : start_lon + rows]
            * wide_values[:, :, start_lon : start_lon + rows]
        )
        lat_rows = [weight[:, start_lon : start_lon + rows] for weight in lat_weights]
        for lat_pos, lat_shift in enumerate(range(1 - HALO, HALO + 1)):
            start_lat = HALO + lat_shift
            weight = lat_rows[lat_pos][None, :, :, start_lat : start_lat + cols]
            term = weight * scaled[:, :, :, start_lat : start_lat + cols]
            total = term if total is None else total + term
    return total


def shards(increment, obs_dep, obs_weight, dep_lon, dep_lat, frac_lon, frac_lat, coupling):
    fields, levels, lon_cells, lat_cells = increment.shape
    nearby = extended_2(increment, (("lon", 2),), HALO, True)
    nearby = extended_2(nearby, (("lat", 3),), HALO, False)
    advected = interpolate(nearby, dep_lon, dep_lat, frac_lon, frac_lat)
    tl_out = column_solve(advected, coupling)
    forcing = obs_weight * (tl_out - obs_dep)
    smoothed = column_solve(forcing, coupling)
    geometry = jnp.stack(
        [dep_lon.astype(jnp.float32), dep_lat.astype(jnp.float32), frac_lon, frac_lat]
    )
    widened = (
        extended_2(smoothed, (("lon", 2),), HALO, True),
        extended_2(geometry, (("lon", 2),), HALO, True),
    )
    widened = (
        extended_2(widened[0], (("lat", 3),), HALO, False),
        extended_2(widened[1], (("lat", 3),), HALO, False),
    )
    wide_values, wide_geometry = widened
    adjoint = collect_own(
        wide_values,
        wide_geometry[0].astype(jnp.int32),
        wide_geometry[1].astype(jnp.int32),
        wide_geometry[2],
        wide_geometry[3],
        lon_cells,
        lat_cells,
    )
    gradient = increment + adjoint
    return (tl_out, gradient)


def solution(mesh):
    placed = (
        P(None, None, "lon", "lat"),
        P(None, None, "lon", "lat"),
        P(None, None, "lon", "lat"),
        P(None, "lon", "lat"),
        P(None, "lon", "lat"),
        P(None, "lon", "lat"),
        P(None, "lon", "lat"),
        P(None, None, "lon", "lat"),
    )
    return jax.shard_map(
        shards,
        mesh=mesh,
        in_specs=placed,
        out_specs=(P(None, None, "lon", "lat"), P(None, None, "lon", "lat")),
        check_vma=False,
    )
```

profile of v0, /device:TPU:0, one launch (start us, length us, event | category | flops | bytes accessed | tf_op | source)
XLA Modules:
  0.0 366.8 jit_solution(16983788367832144045)
XLA Ops:
  3.8 4.0 %collective-permute-start.1 = (f32[4,20,6,128]{3,1,2,0:T(8,128)}, f32[4,20,6,128]{3,1,2,0:T(8,128)S(1)}, u32[]{:S(2)}, u32[]{:S(2)}) collective-permute-start(f32[4,20,6,128]{3,1,2,0:T(8,128)} %copy.1093), channel_id=1, source_target_pairs={{1,0},{2,1},{3,2},{4,3},{5,4},{6,5},{7,6},{0,7},{9,8},{10,9},{11,1... | collective-permute-start | bytes 737288 | tf_op jit(solution)/shard_map/ppermute | solution.py:19
  9.6 4.1 %copy.1072 = f32[4,20,16,128]{2,1,3,0:T(8,128)} copy(f32[4,20,16,128]{3,2,1,0:T(8,128)S(1)} %copy-done.1) | data formatting | bytes 1310720 | tf_op args[0]
  16.6 4.3 %copy.1073 = f32[4,20,6,128]{2,1,3,0:T(8,128)} copy(f32[4,20,6,128]{3,1,2,0:T(8,128)S(1)} %collective-permute-done.1) | data formatting | bytes 491520 | tf_op jit(solution)/shard_map/ppermute | solution.py:19
  20.8 4.2 %copy.1071 = f32[4,20,6,128]{2,1,3,0:T(8,128)} copy(f32[4,20,6,128]{3,1,2,0:T(8,128)S(1)} %collective-permute-done) | data formatting | bytes 491520 | tf_op jit(solution)/shard_map/ppermute | solution.py:17
  25.0 10.0 %pad_maximum_fusion = f32[4,20,28,128]{2,1,3,0:T(8,128)} fusion(f32[4,20,6,128]{2,1,3,0:T(8,128)} %copy.1073, f32[4,20,16,128]{2,1,3,0:T(8,128)} %copy.1072, f32[4,20,6,128]{2,1,3,0:T(8,128)} %copy.1071), kind=kLoop, calls=%fused_computation.260 | loop fusion | flops 573440 | bytes 2293760 | tf_op jit(solution)/shard_map/concatenate | solution.py:15
  35.0 5.6 %copy.1074 = f32[4,20,28,128]{3,2,1,0:T(8,128)} copy(f32[4,20,28,128]{2,1,3,0:T(8,128)} %pad_maximum_fusion) | data formatting | bytes 2293760 | tf_op jit(solution)/shard_map/concatenate | solution.py:15
  43.8 5.3 %collective-permute-start.3 = (f32[4,20,28,6]{2,1,3,0:T(8,128)}, f32[4,20,28,6]{2,1,3,0:T(8,128)}, u32[]{:S(2)}, u32[]{:S(2)}) collective-permute-start(f32[4,20,28,6]{2,1,3,0:T(8,128)} %get-tuple-element.91), channel_id=1, source_target_pairs={{0,8},{8,16},{16,24},{1,9},{9,17},{17,25},{2,10},{10,18},{18,26},{... | collective-permute-start | bytes 161288 | tf_op jit(solution)/shard_map/ppermute | solution.py:17
  53.1 2.7 copy.1081
  58.5 5.4 %collective-permute-start.6 = (f32[4,20,28,6]{2,0,3,1:T(4,128)}, f32[4,20,28,6]{2,0,3,1:T(4,128)}, u32[]{:S(2)}, u32[]{:S(2)}) collective-permute-start(f32[4,20,28,6]{2,0,3,1:T(4,128)} %copy.1080), channel_id=1, source_target_pairs={{0,8},{8,16},{16,24},{1,9},{9,17},{17,25},{2,10},{10,18},{18,26},{... | collective-permute-start | bytes 161288 | tf_op jit(solution)/shard_map/ppermute | solution.py:17
  65.0 2.7 copy.1075
  67.7 2.7 copy.1077
  70.3 136.1 %fusion.11 = f32[4,20,16,128]{3,2,1,0:T(8,128)S(1)} fusion(f32[4,20,16,128]{3,2,1,0:T(8,128)S(1)} %copy-done.1, f32[4,20,6,128]{3,2,1,0:T(8,128)S(1)} %copy.1079, f32[4,20,28,128]{3,2,1,0:T(8,128)} %copy.1074, f32[4,20,28,6]{3,2,1,0:T(8,128)} %copy.1075, f32[4,20,28,6]{3,2,1,0:T(8,128)} %copy.1077, f32[4,20,22,128]{3,2,1,0:T(8,128)S(1)} %copy_dynamic-update-slice_fusion, ...), kind=kLoop, calls=%fused_computation.298 | loop fusion | flops 71598080 | bytes 10019840 | tf_op jit(solution)/shard_map/add | solution.py:77
  210.5 4.1 %copy.1087 = f32[4,20,16,128]{2,1,3,0:T(8,128)} copy(f32[4,20,16,128]{3,2,1,0:T(8,128)S(1)} %constant_dynamic-update-slice_fusion.21) | data formatting | bytes 1310720 | tf_op jit(solution)/shard_map/stack | solution.py:47
  217.8 2.7 pad_maximum_fusion.2
  224.0 2.5 collective-permute-start.9
  252.8 5.3 %copy.1088 = f32[4,20,6,128]{2,1,3,0:T(8,128)} copy(f32[4,20,6,128]{3,1,2,0:T(8,128)} %collective-permute-done.9) | data formatting | bytes 491520 | tf_op jit(solution)/shard_map/ppermute | solution.py:19
  258.0 5.1 %copy.1086 = f32[4,20,6,128]{2,1,3,0:T(8,128)} copy(f32[4,20,6,128]{3,1,2,0:T(8,128)} %collective-permute-done.8) | data formatting | bytes 491520 | tf_op jit(solution)/shard_map/ppermute | solution.py:17
  263.1 8.1 %pad_maximum_fusion.1 = f32[4,20,28,128]{2,1,3,0:T(8,128)S(1)} fusion(f32[4,20,6,128]{2,1,3,0:T(8,128)} %copy.1088, f32[4,20,16,128]{2,1,3,0:T(8,128)} %copy.1087, f32[4,20,6,128]{2,1,3,0:T(8,128)} %copy.1086), kind=kLoop, calls=%fused_computation.261 | loop fusion | flops 573440 | bytes 2293760 | tf_op jit(solution)/shard_map/concatenate | solution.py:15
  271.3 2.6 copy-done
  275.3 5.4 %collective-permute-start.10 = (f32[4,20,28,6]{2,1,3,0:T(8,128)S(1)}, f32[4,20,28,6]{2,1,3,0:T(8,128)}, u32[]{:S(2)}, u32[]{:S(2)}) collective-permute-start(f32[4,20,28,6]{2,1,3,0:T(8,128)S(1)} %get-tuple-element.89), channel_id=1, source_target_pairs={{0,8},{8,16},{16,24},{1,9},{9,17},{17,25},{2,10},{10,18},{18,26},{... | collective-permute-start | bytes 161288 | tf_op jit(solution)/shard_map/ppermute | solution.py:17
  282.5 5.6 %copy.1090 = f32[4,20,28,128]{3,2,1,0:T(8,128)} copy(f32[4,20,28,128]{2,1,3,0:T(8,128)} %copy-done) | data formatting | bytes 2293760 | tf_op jit(solution)/shard_map/concatenate | solution.py:15
  290.4 2.5 pad_maximum_fusion.3
  296.1 4.3 %slice_multiply_fusion.11 = (f32[4,20,16,140]{3,2,1,0:T(8,128)S(1)}, f32[4,20,16,140]{3,2,1,0:T(8,128)S(1)}, f32[4,20,16,140]{3,2,1,0:T(8,128)}, f32[4,20,16,140...) fusion(f32[4,20,28,140]{3,2,1,0:T(8,128)S(1)} %pad_maximum_fusi, ...), kind=kLoop, calls=%fused_computation.285 | loop fusion | flops 1612800 | bytes 14515200 | tf_op jit(solution)/shard_map/mul | solution.py:88
  300.4 66.2 %fusion.415 = f32[4,20,16,128]{3,2,1,0:T(8,128)} fusion(f32[4,20,16,128]{3,2,1,0:T(8,128)S(1)} %copy-done.1, f32[4,20,16,140]{3,2,1,0:T(8,128)S(1)} %get-tuple-element.94, f32[4,20,16,140]{3,2,1,0:T(8,128)} %get-tuple-element.95, f32[4,20,16,140]{3,2,1,0:T(8,128)} %get-tuple-element.96, f32[4,20,16,140]{3,2,1,0:T(8,128)} %get-tuple-element.97, ...), kind=kLoop, calls=%fused_computation.703 | loop fusion | flops 47185920 | bytes 119275520 | tf_op jit(solution)/shard_map/add | solution.py:129
  (166 shorter events, 63.6 us)
Async XLA Ops:
  0.6 7.2 %copy-start.27 = (s32[20,16,128]{2,1,0:T(8,128)S(1)}, s32[20,16,128]{2,1,0:T(8,128)}, u32[]{:S(2)}) copy-start(s32[20,16,128]{2,1,0:T(8,128)} %param.12) | copy-start | bytes 491524
  0.6 7.2 %copy-start.28 = (s32[20,16,128]{2,1,0:T(8,128)S(1)}, s32[20,16,128]{2,1,0:T(8,128)}, u32[]{:S(2)}) copy-start(s32[20,16,128]{2,1,0:T(8,128)} %param.11) | copy-start | bytes 491524
  0.7 7.3 %copy-start.4 = (f32[20,16,128]{2,1,0:T(8,128)S(1)}, f32[20,16,128]{2,1,0:T(8,128)}, u32[]{:S(2)}) copy-start(f32[20,16,128]{2,1,0:T(8,128)} %param.14) | copy-start | bytes 491524
  0.7 7.3 %copy-start.5 = (f32[20,16,128]{2,1,0:T(8,128)S(1)}, f32[20,16,128]{2,1,0:T(8,128)}, u32[]{:S(2)}) copy-start(f32[20,16,128]{2,1,0:T(8,128)} %param.13) | copy-start | bytes 491524
  2.6 18.2 %collective-permute-start = (f32[4,20,6,128]{3,1,2,0:T(8,128)}, f32[4,20,6,128]{3,1,2,0:T(8,128)S(1)}, u32[]{:S(2)}, u32[]{:S(2)}) collective-permute-start(f32[4,20,6,128]{3,1,2,0:T(8,128)} %copy.1092), channel_id=1, source_target_pairs={{0,1},{1,2},{2,3},{3,4},{4,5},{5,6},{6,7},{7,0},{8,9},{9,10},{10,1... | collective-permute-start | bytes 737288 | tf_op jit(solution)/shard_map/ppermute | solution.py:17
  3.8 12.7 %collective-permute-start.1 = (f32[4,20,6,128]{3,1,2,0:T(8,128)}, f32[4,20,6,128]{3,1,2,0:T(8,128)S(1)}, u32[]{:S(2)}, u32[]{:S(2)}) collective-permute-start(f32[4,20,6,128]{3,1,2,0:T(8,128)} %copy.1093), channel_id=1, source_target_pairs={{1,0},{2,1},{3,2},{4,3},{5,4},{6,5},{7,6},{0,7},{9,8},{10,9},{11,1... | collective-permute-start | bytes 737288 | tf_op jit(solution)/shard_map/ppermute | solution.py:19
  7.9 41.9 %copy-start.6 = (f32[1,20,16,128]{3,2,1,0:T(8,128)}, f32[1,20,16,128]{3,2,1,0:T(8,128)S(1)}, u32[]{:S(2)}) copy-start(f32[1,20,16,128]{3,2,1,0:T(8,128)S(1)} %get-tuple-element.319) | copy-start | bytes 491524
  8.9 40.2 %collective-permute-start.5 = (f32[4,20,6,128]{3,2,1,0:T(8,128)}, f32[4,20,6,128]{3,2,1,0:T(8,128)S(1)}, u32[]{:S(2)}, u32[]{:S(2)}) collective-permute-start(f32[4,20,6,128]{3,2,1,0:T(8,128)} %get-tuple-element.290), channel_id=1, source_target_pairs={{1,0},{2,1},{3,2},{4,3},{5,4},{6,5},{7,6},{0,7},{9,8},{10,9},{11,1... | collective-permute-start | bytes 737288 | tf_op jit(solution)/shard_map/ppermute | solution.py:19
  9.5 40.2 %collective-permute-start.4 = (f32[4,20,6,128]{3,2,1,0:T(8,128)}, f32[4,20,6,128]{3,2,1,0:T(8,128)}, u32[]{:S(2)}, u32[]{:S(2)}) collective-permute-start(f32[4,20,6,128]{3,2,1,0:T(8,128)} %get-tuple-element.289), channel_id=1, source_target_pairs={{0,1},{1,2},{2,3},{3,4},{4,5},{5,6},{6,7},{7,0},{8,9},{9,10},{10,1... | collective-permute-start | bytes 737288 | tf_op jit(solution)/shard_map/ppermute | solution.py:17
  16.6 4.3 %copy-start.24 = (f32[4,20,6,128]{3,1,2,0:T(8,128)}, f32[4,20,6,128]{3,1,2,0:T(8,128)S(1)}, u32[]{:S(2)}) copy-start(f32[4,20,6,128]{3,1,2,0:T(8,128)S(1)} %collective-permute-done.1) | copy-start | bytes 737284
  20.8 4.2 %copy-start.23 = (f32[4,20,6,128]{3,1,2,0:T(8,128)}, f32[4,20,6,128]{3,1,2,0:T(8,128)S(1)}, u32[]{:S(2)}) copy-start(f32[4,20,6,128]{3,1,2,0:T(8,128)S(1)} %collective-permute-done) | copy-start | bytes 737284
  42.5 22.5 %collective-permute-start.2 = (f32[4,20,28,6]{2,1,3,0:T(8,128)}, f32[4,20,28,6]{2,1,3,0:T(8,128)}, u32[]{:S(2)}, u32[]{:S(2)}) collective-permute-start(f32[4,20,28,6]{2,1,3,0:T(8,128)} %get-tuple-element.92), channel_id=1, source_target_pairs={{8,0},{16,8},{24,16},{9,1},{17,9},{25,17},{10,2},{18,10},{26,18},{... | collective-permute-start | bytes 161288 | tf_op jit(solution)/shard_map/ppermute | solution.py:19
  43.8 23.9 %collective-permute-start.3 = (f32[4,20,28,6]{2,1,3,0:T(8,128)}, f32[4,20,28,6]{2,1,3,0:T(8,128)}, u32[]{:S(2)}, u32[]{:S(2)}) collective-permute-start(f32[4,20,28,6]{2,1,3,0:T(8,128)} %get-tuple-element.91), channel_id=1, source_target_pairs={{0,8},{8,16},{16,24},{1,9},{9,17},{17,25},{2,10},{10,18},{18,26},{... | collective-permute-start | bytes 161288 | tf_op jit(solution)/shard_map/ppermute | solution.py:17
  53.1 4.0 %copy-start.3 = (f32[4,20,28,6]{3,2,1,0:T(8,128)S(1)}, f32[4,20,28,6]{3,2,1,0:T(8,128)}, u32[]{:S(2)}) copy-start(f32[4,20,28,6]{3,2,1,0:T(8,128)} %get-tuple-element.143) | copy-start | bytes 161284
  53.1 10.8 %copy-start.25 = (f32[4,20,6,128]{3,1,2,0:T(8,128)S(1)}, f32[4,20,6,128]{3,1,2,0:T(8,128)}, u32[]{:S(2)}) copy-start(f32[4,20,6,128]{3,1,2,0:T(8,128)} %copy-done.24) | copy-start | bytes 737284
  55.9 158.7 %collective-permute-start.7 = (f32[4,20,28,6]{2,0,3,1:T(4,128)}, f32[4,20,28,6]{2,0,3,1:T(4,128)}, u32[]{:S(2)}, u32[]{:S(2)}) collective-permute-start(f32[4,20,28,6]{2,0,3,1:T(4,128)} %copy.1081), channel_id=1, source_target_pairs={{8,0},{16,8},{24,16},{9,1},{17,9},{25,17},{10,2},{18,10},{26,18},{... | collective-permute-start | bytes 161288 | tf_op jit(solution)/shard_map/ppermute | solution.py:19
  58.5 157.7 %collective-permute-start.6 = (f32[4,20,28,6]{2,0,3,1:T(4,128)}, f32[4,20,28,6]{2,0,3,1:T(4,128)}, u32[]{:S(2)}, u32[]{:S(2)}) collective-permute-start(f32[4,20,28,6]{2,0,3,1:T(4,128)} %copy.1080), channel_id=1, source_target_pairs={{0,8},{8,16},{16,24},{1,9},{9,17},{17,25},{2,10},{10,18},{18,26},{... | collective-permute-start | bytes 161288 | tf_op jit(solution)/shard_map/ppermute | solution.py:17
  70.3 136.1 %copy-start.2 = (f32[4,19,16,128]{3,2,1,0:T(8,128)S(1)}, f32[4,19,16,128]{3,2,1,0:T(8,128)}, u32[]{:S(2)}) copy-start(f32[4,19,16,128]{3,2,1,0:T(8,128)} %param.15) | copy-start | bytes 1867780
  223.0 3.5 copy-start.12
  224.0 28.7 %collective-permute-start.9 = (f32[4,20,6,128]{3,1,2,0:T(8,128)S(1)}, f32[4,20,6,128]{3,1,2,0:T(8,128)}, u32[]{:S(2)}, u32[]{:S(2)}) collective-permute-start(f32[4,20,6,128]{3,1,2,0:T(8,128)S(1)} %copy.1095), channel_id=1, source_target_pairs={{1,0},{2,1},{3,2},{4,3},{5,4},{6,5},{7,6},{0,7},{9,8},{10,9},{11,1... | collective-permute-start | bytes 737288 | tf_op jit(solution)/shard_map/ppermute | solution.py:19
  227.2 30.8 %collective-permute-start.8 = (f32[4,20,6,128]{3,1,2,0:T(8,128)}, f32[4,20,6,128]{3,1,2,0:T(8,128)}, u32[]{:S(2)}, u32[]{:S(2)}) collective-permute-start(f32[4,20,6,128]{3,1,2,0:T(8,128)} %copy.1094), channel_id=1, source_target_pairs={{0,1},{1,2},{2,3},{3,4},{4,5},{5,6},{6,7},{7,0},{8,9},{9,10},{10,1... | collective-permute-start | bytes 737288 | tf_op jit(solution)/shard_map/ppermute | solution.py:17
  274.0 14.2 %collective-permute-start.11 = (f32[4,20,28,6]{2,1,3,0:T(8,128)S(1)}, f32[4,20,28,6]{2,1,3,0:T(8,128)S(1)}, u32[]{:S(2)}, u32[]{:S(2)}) collective-permute-start(f32[4,20,28,6]{2,1,3,0:T(8,128)S(1)} %get-tuple-element.90), channel_id=1, source_target_pairs={{8,0},{16,8},{24,16},{9,1},{17,9},{25,17},{10,2},{18,10},{26,18},{... | collective-permute-start | bytes 161288 | tf_op jit(solution)/shard_map/ppermute | solution.py:19
  275.3 13.5 %collective-permute-start.10 = (f32[4,20,28,6]{2,1,3,0:T(8,128)S(1)}, f32[4,20,28,6]{2,1,3,0:T(8,128)}, u32[]{:S(2)}, u32[]{:S(2)}) collective-permute-start(f32[4,20,28,6]{2,1,3,0:T(8,128)S(1)} %get-tuple-element.89), channel_id=1, source_target_pairs={{0,8},{8,16},{16,24},{1,9},{9,17},{17,25},{2,10},{10,18},{18,26},{... | collective-permute-start | bytes 161288 | tf_op jit(solution)/shard_map/ppermute | solution.py:17
  292.9 3.1 copy-start.22
  (19 other events, 36.6 us)
where the time goes:
time: 373 us; the launch traced here: 367 us
  other arithmetic  245 us (66%)
  local copies, waits for them, and re-layouts  92 us (25%)
  starting transfers between devices  28 us (8%)
    add x1, other arithmetic, interpolate(): total = term if total is None else total + term  136 us
    add x1, other arithmetic, shards(): gradient = increment + adjoint  66.2 us
    concatenate x5, other arithmetic, extended_2(): jnp.concatenate([lax.ppermute(tail, axis, [(i, (i + 1) % count) for i in...  24.7 us
    slice x12, local copies, waits for them, and re-layouts, collect_own(): weight = lat_rows[lat_pos][None, :, :, start_lat:start_lat + cols]  22 us
    ppermute x6, starting transfers between devices, extended_2(): lax.ppermute(tail, axis, [(i, (i + 1) % count) for i in range(ends)])  17 us
    ppermute x6, local copies, waits for them, and re-layouts, extended_2(): lax.ppermute(tail, axis, [(i, (i + 1) % count) for i in range(ends)])  16.2 us
    ppermute x5, local copies, waits for them, and re-layouts, extended_2(): lax.ppermute(head, axis, [((i + 1) % count, i) for i in range(ends)])  14.4 us
    unnamed x86, local copies, waits for them, and re-layouts  13.2 us
  transfers between devices with their start and end apart: 12, of which 0 were waited for; matrix products, arithmetic and copies ran while one was open for 63% of the time, Pallas kernels for 0%

commit v1 on v0

v1 whole, which is shorter than its diff:
```python
import functools

import jax
import jax.numpy as jnp
from jax import lax
from jax.experimental import pallas as pl
from jax.experimental.pallas import tpu as pltpu
from jax.sharding import PartitionSpec as P

HALO = 6
SHIFTS = tuple(range(1 - HALO, HALO + 1))
LANES = 128
SLOT = 16
PER = LANES // SLOT
MESH = pl.DeviceIdType.MESH
ANY = pl.BlockSpec(memory_space=pl.ANY)
VMEM = pl.BlockSpec(memory_space=pltpu.VMEM)
LIMIT = 56 * 1024 * 1024


def lane_index(shape):
    return lax.broadcasted_iota(jnp.int32, shape, len(shape) - 1)


def roll(x, shift):
    return pltpu.roll(x, shift, x.ndim - 1)


def neighbours(sizes):
    lat, lon = lax.axis_index("lat"), lax.axis_index("lon")

    def at(dy, dx):
        return {
            "lat": lax.rem(lat + dy + sizes[0], sizes[0]),
            "lon": lax.rem(lon + dx + sizes[1], sizes[1]),
        }

    return at


def greet(devices):
    barrier = pltpu.get_barrier_semaphore()
    for device in devices:
        pl.semaphore_signal(barrier, inc=1, device_id=device, device_id_type=MESH)
    pl.semaphore_wait(barrier, len(devices))


def remote(src, dst, send, recv, number, device):
    return pltpu.make_async_remote_copy(
        src_ref=src,
        dst_ref=dst,
        send_sem=send.at[number],
        recv_sem=recv.at[number],
        device_id=device,
        device_id_type=MESH,
    )


def pack_edges(src, dst):
    @pl.loop(0, dst.shape[0])
    def _(group):
        total = None
        for e in range(PER):
            x = src[group * PER + e]
            lane = lane_index(x.shape)
            x = jnp.where((lane < HALO) | (lane >= LANES - HALO), x, 0.0)
            x = roll(x, (HALO + SLOT * e) % LANES)
            total = x if total is None else total + x
        dst[group] = total


def increment_exchange(sizes, inc, from_left, from_right, edges, local, packed, send, recv, here):
    at = neighbours(sizes)
    own = pltpu.make_async_copy(inc, local, here)
    own.start()
    greet([at(dy, dx) for dy in (-1, 0, 1) for dx in (-1, 0, 1) if (dy, dx) != (0, 0)])
    copies = [
        remote(inc.at[:, 0:8], from_right, send, recv, 0, at(0, -1)),
        remote(inc.at[:, 8:16], from_left, send, recv, 1, at(0, 1)),
    ]
    for copy in copies:
        copy.start()
    own.wait()
    pack_edges(local, packed)
    number = 2
    for dy in (-1, 1):
        side = 0 if dy == 1 else 1
        for dx in (0, -1, 1):
            rows, into = {0: ((0, 16), 8), -1: ((0, 8), 24), 1: ((8, 16), 0)}[dx]
            copy = remote(
                packed.at[:, rows[0] : rows[1]],
                edges.at[side, :, into : into + rows[1] - rows[0]],
                send,
                recv,
                number,
                at(dy, dx),
            )
            copy.start()
            copies.append(copy)
            number += 1
    for copy in copies:
        copy.wait()


def sector_exchange(sizes, z, from_left, from_right, send, recv):
    at = neighbours(sizes)
    greet([at(0, -1), at(0, 1)])
    copies = [
        remote(z.at[:, 0:8], from_right, send, recv, 0, at(0, -1)),
        remote(z.at[:, 8:16], from_left, send, recv, 1, at(0, 1)),
    ]
    for copy in copies:
        copy.start()
    for copy in copies:
        copy.wait()


def band_exchange(sizes, packed, edges, send, recv):
    at = neighbours(sizes)
    greet([at(-1, 0), at(1, 0)])
    copies = [
        remote(packed, edges.at[1], send, recv, 0, at(-1, 0)),
        remote(packed, edges.at[0], send, recv, 1, at(1, 0)),
    ]
    for copy in copies:
        copy.start()
    for copy in copies:
        copy.wait()


def store_weights(dst, offset, frac):
    rest = 1.0 - frac
    before = None
    for pos, total in enumerate(SHIFTS):
        here = offset == total
        second = 0.0 if before is None else jnp.where(before, frac, 0.0)
        dst[pos] = jnp.where(here, rest, second)
        before = here


def forward_kernel(
    dims, bands, inc, from_left, from_right, edges, dep, weight, olon, olat, flon, flat, coup,
    tl, z, shifted, lonw, latw, prime, ratio, inverse,
):
    fields, levels = dims
    band = lax.axis_index("lat")
    has_lower = band > 0
    has_upper = band < bands - 1

    @pl.loop(0, levels)
    def _(k):
        store_weights(lonw, olon[k], flon[k])
        store_weights(latw, olat[k], flat[k])

        @pl.loop(0, fields)
        def _(f):
            at = f * levels + k
            main = jnp.concatenate([from_left[at], inc[at], from_right[at]], axis=0)
            group, slot = at // PER, at % PER
            shift = lax.rem(2 * LANES - HALO - SLOT * slot, LANES)
            lane = lane_index(main.shape)
            lower = jnp.where(has_lower, roll(edges[0, group], shift), 0.0)
            upper = jnp.where(has_upper, roll(edges[1, group], shift), 0.0)
            edge = jnp.where(lane < LANES // 2, upper, lower)
            for pos, total in enumerate(SHIFTS):
                t = -total
                if t == 0:
                    shifted[pos] = main
                    continue
                inside = (lane >= LANES + t) if t < 0 else (lane < t)
                shifted[pos] = roll(jnp.where(inside, edge, main), (-t) % LANES)
            c = f * (levels - 1) + k
            first, last = k == 0, k == levels - 1
            for half in range(2):
                rows = pl.ds(8 * half, 8)
                lat = [latw[pos, rows] for pos in range(len(SHIFTS))]
                adv = None
                for lon_pos, lon_total in enumerate(SHIFTS):
                    inner = None
                    start = 8 + 8 * half - lon_total
                    for pos in range(len(SHIFTS)):
                        term = lat[pos] * shifted[pos, pl.ds(start, 8)]
                        inner = term if inner is None else inner + term
                    term = lonw[lon_pos, rows] * inner
                    adv = term if adv is None else adv + term
                below = jnp.where(first, 0.0, coup[jnp.where(first, c, c - 1), rows])
                above = jnp.where(last, 0.0, coup[jnp.where(last, c - 1, c), rows])
                prev = jnp.where(first, at, at - 1)
                ratio_prev = jnp.where(first, 0.0, ratio[prev, rows])
                prime_prev = jnp.where(first, 0.0, prime[prev, rows])
                inv = 1.0 / (1.0 + below + above - below * ratio_prev)
                inverse[at, rows] = inv
                ratio[at, rows] = above * inv
                prime[at, rows] = (adv + below * prime_prev) * inv

    @pl.loop(0, fields)
    def _(f):
        base = f * levels
        x = prime[base + levels - 1]
        tl[base + levels - 1] = x
        for k in range(levels - 2, -1, -1):
            x = prime[base + k] + ratio[base + k] * x
            tl[base + k] = x
        kept = []
        for k in range(levels):
            at = base + k
            forcing = weight[at] * (tl[at] - dep[at])
            if k > 0:
                forcing = forcing + coup[f * (levels - 1) + k - 1] * kept[-1]
            kept.append(forcing * inverse[at])
        x = kept[-1]
        z[base + levels - 1] = x
        for k in range(levels - 2, -1, -1):
            x = kept[k] + ratio[base + k] * x
            z[base + k] = x


def adjoint_kernel(
    dims, inc, z, z_left, z_right, olon, olat, flon, flat, g_left, g_right,
    grad, packed, lonw, latw, wide, spill,
):
    fields, levels = dims
    lane = lane_index((8, LANES))

    def widened(own, number, k):
        left, right = g_left[number, k], g_right[number, k]
        return jnp.concatenate([left, own[k].astype(jnp.float32), right], axis=0)

    @pl.loop(0, levels)
    def _(k):
        store_weights(lonw, widened(olon, 0, k), widened(flon, 2, k))
        store_weights(latw, widened(olat, 1, k), widened(flat, 3, k))
        for f in range(fields):
            at = f * levels + k
            wide[f, 0:8] = z_left[at]
            wide[f, 8:24] = z[at]
            wide[f, 24:32] = z_right[at]
        for half in range(2):
            rows = pl.ds(8 * half, 8)
            for pair in range(0, fields, 2):
                both = range(pair, min(pair + 2, fields))
                sums = {}
                for lon_pos, lon_total in enumerate(SHIFTS):
                    near = pl.ds(8 + 8 * half + lon_total, 8)
                    scale = lonw[lon_pos, near]
                    scaled = {f: scale * wide[f, near] for f in both}
                    for pos in range(len(SHIFTS)):
                        w = latw[pos, near]
                        for f in both:
                            term = w * scaled[f]
                            sums[f, pos] = term if lon_pos == 0 else sums[f, pos] + term
                for f in both:
                    at = f * levels + k
                    total, outside = inc[at, rows], jnp.zeros((8, LANES), jnp.float32)
                    for pos, n in enumerate(SHIFTS):
                        if n == 0:
                            total = total + sums[f, pos]
                            continue
                        moved = roll(sums[f, pos], (-n) % LANES)
                        wraps = (lane >= LANES - n) if n > 0 else (lane < -n)
                        total = total + jnp.where(wraps, 0.0, moved)
                        outside = outside + jnp.where(wraps, moved, 0.0)
                    grad[at, rows] = total
                    spill[at, rows] = outside

    pack_edges(spill, packed)


def finish_kernel(bands, partial, edges, grad):
    band = lax.axis_index("lat")
    has_lower = band > 0
    has_upper = band < bands - 1
    lane = lane_index(partial.shape[1:])

    @pl.loop(0, edges.shape[1])
    def _(group):
        both = edges[0, group], edges[1, group]
        lower = jnp.where(has_lower, both[0], 0.0)
        upper = jnp.where(has_upper, both[1], 0.0)
        for e in range(PER):
            shift = (-HALO - SLOT * e) % LANES
            low = jnp.where(lane < HALO, roll(lower, shift), 0.0)
            high = jnp.where(lane >= LANES - HALO, roll(upper, shift), 0.0)
            at = group * PER + e
            grad[at] = partial[at] + (low + high)


def shards(sizes, increment, obs_dep, obs_weight, dep_lon, dep_lat, frac_lon, frac_lat, coupling):
    fields, levels, rows, cols = increment.shape
    count = fields * levels
    groups = count // PER
    dims = (fields, levels)
    f32 = jnp.float32

    def shape(*s):
        return jax.ShapeDtypeStruct(s, f32)

    def flat3(x):
        return x.reshape(-1, rows, cols)

    inc, dep, weight, coup = flat3(increment), flat3(obs_dep), flat3(obs_weight), flat3(coupling)
    tile = shape(count, 8, cols)
    whole = shape(count, rows, cols)

    from_left, from_right, edges = pl.pallas_call(
        functools.partial(increment_exchange, sizes),
        out_shape=(tile, tile, shape(2, groups, 32, cols)),
        in_specs=[ANY],
        out_specs=(ANY,) * 3,
        scratch_shapes=[
            pltpu.VMEM((count, rows, cols), f32),
            pltpu.VMEM((groups, rows, cols), f32),
            pltpu.SemaphoreType.DMA((8,)),
            pltpu.SemaphoreType.DMA((8,)),
            pltpu.SemaphoreType.DMA,
        ],
        compiler_params=pltpu.CompilerParams(collective_id=0, has_side_effects=True),
    )(inc)

    geometry = jnp.stack([dep_lon.astype(f32), dep_lat.astype(f32), frac_lon, frac_lat])
    n = sizes[1]
    g_left = lax.ppermute(geometry[:, :, 8:16], "lon", [(i, (i + 1) % n) for i in range(n)])
    g_right = lax.ppermute(geometry[:, :, 0:8], "lon", [((i + 1) % n, i) for i in range(n)])

    tl, z = pl.pallas_call(
        functools.partial(forward_kernel, dims, sizes[0]),
        out_shape=(whole, whole),
        in_specs=[VMEM] * 11,
        out_specs=(VMEM,) * 2,
        scratch_shapes=[
            pltpu.VMEM((12, 32, cols), f32),
            pltpu.VMEM((12, rows, cols), f32),
            pltpu.VMEM((12, rows, cols), f32),
            pltpu.VMEM((count, rows, cols), f32),
            pltpu.VMEM((count, rows, cols), f32),
            pltpu.VMEM((count, rows, cols), f32),
        ],
        compiler_params=pltpu.CompilerParams(vmem_limit_bytes=LIMIT),
        cost_estimate=pl.CostEstimate(flops=60_000_000, bytes_accessed=8_000_000, transcendentals=0),
    )(inc, from_left, from_right, edges, dep, weight, dep_lon, dep_lat, frac_lon, frac_lat, coup)

    z_left, z_right = pl.pallas_call(
        functools.partial(sector_exchange, sizes),
        out_shape=(tile, tile),
        in_specs=[ANY],
        out_specs=(ANY,) * 2,
        scratch_shapes=[pltpu.SemaphoreType.DMA((2,)), pltpu.SemaphoreType.DMA((2,))],
        compiler_params=pltpu.CompilerParams(collective_id=1, has_side_effects=True),
    )(z)

    partial, packed = pl.pallas_call(
        functools.partial(adjoint_kernel, dims),
        out_shape=(whole, shape(groups, rows, cols)),
        in_specs=[VMEM] * 10,
        out_specs=(VMEM,) * 2,
        scratch_shapes=[
            pltpu.VMEM((12, 32, cols), f32),
            pltpu.VMEM((12, 32, cols), f32),
            pltpu.VMEM((fields, 32, cols), f32),
            pltpu.VMEM((count, rows, cols), f32),
        ],
        compiler_params=pltpu.CompilerParams(vmem_limit_bytes=LIMIT),
    )(inc, z, z_left, z_right, dep_lon, dep_lat, frac_lon, frac_lat, g_left, g_right)

    back = pl.pallas_call(
        functools.partial(band_exchange, sizes),
        out_shape=shape(2, groups, rows, cols),
        in_specs=[ANY],
        out_specs=ANY,
        scratch_shapes=[pltpu.SemaphoreType.DMA((2,)), pltpu.SemaphoreType.DMA((2,))],
        compiler_params=pltpu.CompilerParams(collective_id=2, has_side_effects=True),
    )(packed)

    grad = pl.pallas_call(
        functools.partial(finish_kernel, sizes[0]),
        out_shape=whole,
        in_specs=[VMEM] * 2,
        out_specs=VMEM,
        compiler_params=pltpu.CompilerParams(vmem_limit_bytes=LIMIT),
    )(partial, back)
    return tl.reshape(increment.shape), grad.reshape(increment.shape)


def solution(mesh):
    sizes = (mesh.shape["lat"], mesh.shape["lon"])
    wide = P(None, None, "lon", "lat")
    level = P(None, "lon", "lat")
    return jax.shard_map(
        functools.partial(shards, sizes),
        mesh=mesh,
        in_specs=(wide, wide, wide, level, level, level, level, wide),
        out_specs=(wide, wide),
        check_vma=False,
    )
```

time: 373 us -> 86.8 us (0.23); the launches traced: 367 us -> 86.6 us
  other arithmetic: 245 us -> 1.11 us
  local copies, waits for them, and re-layouts: 92 us -> 0.94 us
  Pallas kernels: 0 us -> 79.3 us
  starting transfers between devices: 28 us -> 4.54 us
    add x9 -> x0, other arithmetic: 211 us -> none  [the longest x1 136 us: interpolate(): total = term if total is None else total + term]
    pallas_call x0 -> x6, Pallas kernels: none -> 79.3 us  [the longest x1 25.1 us: shards(): pl.pallas_call(functools.partial(forward_kernel, dims, sizes[0]), out_sha...]
    slice x20 -> x1, local copies, waits for them, and re-layouts: 33 us -> 0.04 us  [shards(): geometry[:, :, 0:8]]
    ppermute x11 -> x0, local copies, waits for them, and re-layouts: 30.5 us -> none  [the longest x6 16.2 us: extended_2(): lax.ppermute(tail, axis, [(i, (i + 1) % count) for i in range(ends)])]
    concatenate x5 -> x0, other arithmetic: 24.7 us -> none  [extended_2(): jnp.concatenate([lax.ppermute(tail, axis, [(i, (i + 1) % count) for i in...]
    ppermute x12 -> x2, starting transfers between devices: 28 us -> 4.54 us  [the longest x1 4.54 us: shards(): lax.ppermute(geometry[:, :, 0:8], 'lon', [((i + 1) % n, i) for i in range...]
    unnamed x86 -> x8, local copies, waits for them, and re-layouts: 13.2 us -> 0.9 us
    concatenate x3 -> x0, local copies, waits for them, and re-layouts: 11.2 us -> none  [extended_2(): jnp.concatenate([lax.ppermute(tail, axis, [(i, (i + 1) % count) for i in...]
  transfers between devices with their start and end apart: 12 -> 2, of which waited for: 0 -> 0; matrix products, arithmetic and copies ran while one was open for 63% -> 0% of each run, Pallas kernels for 0% -> 64%
where the time goes in v1:
time: 86.8 us; the launch traced here: 86.6 us
  Pallas kernels  79.3 us (91%)
  starting transfers between devices  4.54 us (5%)
  other arithmetic  1.11 us (1%)
  local copies, waits for them, and re-layouts  0.94 us (1%)
    pallas_call x1, Pallas kernels, shards(): pl.pallas_call(functools.partial(forward_kernel, dims, sizes[0]), out_sha...  25.1 us
    pallas_call x1, Pallas kernels, shards(): pl.pallas_call(functools.partial(increment_exchange, sizes), out_shape=(t...  20 us
    pallas_call x1, Pallas kernels, shards(): pl.pallas_call(functools.partial(adjoint_kernel, dims), out_shape=(whole,...  14.2 us
    pallas_call x1, Pallas kernels, shards(): pl.pallas_call(functools.partial(sector_exchange, sizes), out_shape=(tile...  10.4 us
    pallas_call x1, Pallas kernels, shards(): pl.pallas_call(functools.partial(band_exchange, sizes), out_shape=shape(2...  6.57 us
    ppermute x1, starting transfers between devices, shards(): lax.ppermute(geometry[:, :, 0:8], 'lon', [((i + 1) % n, i) for i in range...  4.54 us
    pallas_call x1, Pallas kernels, shards(): pl.pallas_call(functools.partial(finish_kernel, sizes[0]), out_shape=whol...  2.99 us
  transfers between devices with their start and end apart: 2, of which 0 were waited for; matrix products, arithmetic and copies ran while one was open for 0% of the time, Pallas kernels for 64%

profile of v1, /device:TPU:0, one launch (start us, length us, event | category | flops | bytes accessed | tf_op | source)
XLA Modules:
  0.0 86.6 jit_solution(16240971997837974746)
XLA Ops:
  0.6 0.0 copy-start
  0.6 0.0 copy-start.1
  0.7 1.1 %convert_bitcast_fusion = (f32[1,20,16,128]{3,2,1,0:T(8,128)S(1)}, f32[1,20,16,128]{3,2,1,0:T(8,128)S(1)}) fusion(s32[20,16,128]{2,1,0:T(8,128)} %olat.3, s32[20,16,128]{2,1,0:T(8,128)} %olon.3), kind=kLoop, calls=%fused_computation.1 | loop fusion | flops 81920 | bytes 655360 | tf_op jit(solution)/shard_map/stack | solution.py:320
  1.7 0.0 copy-done
  1.7 0.1 copy-done.1
  1.9 4.5 %collective-permute-start.1 = (f32[4,20,8,128]{3,2,1,0:T(8,128)S(1)}, f32[4,20,8,128]{3,2,1,0:T(8,128)S(1)}, u32[]{:S(2)}, u32[]{:S(2)}) collective-permute-start(f32[4,20,8,128]{3,2,1,0:T(8,128)S(1)} %get-tuple-element.20), channel_id=1, source_target_pairs={{1,0},{2,1},{3,2},{4,3},{5,4},{6,5},{7,6},{0,7},{9,8},{10,9},{11,1... | collective-permute-start | bytes 983048 | tf_op jit(solution)/shard_map/ppermute | solution.py:323
  6.4 0.0 collective-permute-start
  6.4 20.0 %shard_map.95 = (f32[80,8,128]{2,1,0:T(8,128)}, f32[80,8,128]{2,1,0:T(8,128)}, f32[2,10,32,128]{3,2,1,0:T(8,128)}) custom-call(f32[80,16,128]{2,1,0:T(8,128)} %bitcast.12), custom_call_target="tpu_custom_call" | custom-call | tf_op jit(solution)/shard_map/pallas_call | solution.py:305
  26.5 25.1 %shard_map.96 = (f32[80,16,128]{2,1,0:T(8,128)}, f32[80,16,128]{2,1,0:T(8,128)}) custom-call(f32[80,16,128]{2,1,0:T(8,128)} %bitcast.13, f32[80,8,128]{2,1,0:T(8,128)} %get-tuple-element.11.from_left, f32[80,8,128]{2,1,0:T(8,128)} %get-tuple-element.12.from_right, f32[2,10,32,128]{3,2,1,0:T(8,128)} %get-tuple-element.13.edges, f32[80,16,128]{2,1,0:T(8,128)} %bitcast.18, ...), custom_call_target="tpu_custom_call" | custom-call | flops 60000000 | bytes 8000000 | tf_op jit(solution)/shard_map/pallas_call | solution.py:325
  51.6 10.4 %shard_map.97 = (f32[80,8,128]{2,1,0:T(8,128)}, f32[80,8,128]{2,1,0:T(8,128)}) custom-call(f32[80,16,128]{2,1,0:T(8,128)} %get-tuple-element.15.z), custom_call_target="tpu_custom_call" | custom-call | tf_op jit(solution)/shard_map/pallas_call | solution.py:342
  62.0 0.0 collective-permute-done.1.g_right
  62.0 0.0 copy-start.2
  62.0 0.0 collective-permute-done.g_left
  62.0 0.0 copy-start.3
  62.0 0.7 copy-done.2
  62.7 0.1 copy-done.3
  62.9 14.2 %shard_map.98 = (f32[80,16,128]{2,1,0:T(8,128)}, f32[10,16,128]{2,1,0:T(8,128)}) custom-call(f32[80,16,128]{2,1,0:T(8,128)} %bitcast.14, f32[80,16,128]{2,1,0:T(8,128)} %get-tuple-element.15.z, f32[80,8,128]{2,1,0:T(8,128)} %get-tuple-element.16.z_left, f32[80,8,128]{2,1,0:T(8,128)} %get-tuple-element.17.z_right, s32[20,16,128]{2,1,0:T(8,128)} %olon.3, ...), custom_call_target="tpu_custom_call" | custom-call | tf_op jit(solution)/shard_map/pallas_call | solution.py:351
  77.0 6.6 %shard_map.99.edges = f32[2,10,16,128]{3,2,1,0:T(8,128)} custom-call(f32[10,16,128]{2,1,0:T(8,128)} %get-tuple-element.19.packed), custom_call_target="tpu_custom_call" | custom-call | tf_op jit(solution)/shard_map/pallas_call | solution.py:365
  83.6 3.0 %shard_map.100 = f32[80,16,128]{2,1,0:T(8,128)} custom-call(f32[80,16,128]{2,1,0:T(8,128)} %get-tuple-element.18.partial, f32[2,10,16,128]{3,2,1,0:T(8,128)} %shard_map.99.edges), custom_call_target="tpu_custom_call" | custom-call | tf_op jit(solution)/shard_map/pallas_call | solution.py:374
  (2 shorter events, 0.1 us)
Async XLA Ops:
  0.6 1.1 %copy-start = (f32[20,16,128]{2,1,0:T(8,128)S(1)}, f32[20,16,128]{2,1,0:T(8,128)}, u32[]{:S(2)}) copy-start(f32[20,16,128]{2,1,0:T(8,128)} %flon.3) | copy-start | bytes 491524
  0.6 1.1 %copy-start.1 = (f32[20,16,128]{2,1,0:T(8,128)S(1)}, f32[20,16,128]{2,1,0:T(8,128)}, u32[]{:S(2)}) copy-start(f32[20,16,128]{2,1,0:T(8,128)} %flat.3) | copy-start | bytes 491524
  1.9 60.1 %collective-permute-start.1 = (f32[4,20,8,128]{3,2,1,0:T(8,128)S(1)}, f32[4,20,8,128]{3,2,1,0:T(8,128)S(1)}, u32[]{:S(2)}, u32[]{:S(2)}) collective-permute-start(f32[4,20,8,128]{3,2,1,0:T(8,128)S(1)} %get-tuple-element.20), channel_id=1, source_target_pairs={{1,0},{2,1},{3,2},{4,3},{5,4},{6,5},{7,6},{0,7},{9,8},{10,9},{11,1... | collective-permute-start | bytes 983048 | tf_op jit(solution)/shard_map/ppermute | solution.py:323
  6.4 55.6 %collective-permute-start = (f32[4,20,8,128]{3,2,1,0:T(8,128)S(1)}, f32[4,20,8,128]{3,2,1,0:T(8,128)S(1)}, u32[]{:S(2)}, u32[]{:S(2)}) collective-permute-start(f32[4,20,8,128]{3,2,1,0:T(8,128)S(1)} %get-tuple-element.21), channel_id=1, source_target_pairs={{0,1},{1,2},{2,3},{3,4},{4,5},{5,6},{6,7},{7,0},{8,9},{9,10},{10,1... | collective-permute-start | bytes 983048 | tf_op jit(solution)/shard_map/ppermute | solution.py:322
  62.0 0.7 copy-start.2
  62.0 0.8 copy-start.3

commit v2 on v1

v2 whole, which is shorter than its diff:
```python
import functools

import jax
import jax.numpy as jnp
from jax import lax
from jax.experimental import pallas as pl
from jax.experimental.pallas import tpu as pltpu
from jax.sharding import PartitionSpec as P

HALO = 6
SHIFTS = tuple(range(1 - HALO, HALO + 1))
LANES = 128
SLOT = 16
PER = LANES // SLOT
QUAD = 4
PAIR = 2
MESH = pl.DeviceIdType.MESH
ANY = pl.BlockSpec(memory_space=pl.ANY)
LIMIT = 56 * 1024 * 1024


def lane_index(shape):
    return lax.broadcasted_iota(jnp.int32, shape, len(shape) - 1)


def roll(x, shift):
    return pltpu.roll(x, shift, x.ndim - 1)


def neighbours(sizes):
    lat, lon = lax.axis_index("lat"), lax.axis_index("lon")

    def at(dy, dx):
        return {
            "lat": lax.rem(lat + dy + sizes[0], sizes[0]),
            "lon": lax.rem(lon + dx + sizes[1], sizes[1]),
        }

    return at


def greet(devices):
    barrier = pltpu.get_barrier_semaphore()
    for device in devices:
        pl.semaphore_signal(barrier, inc=1, device_id=device, device_id_type=MESH)
    pl.semaphore_wait(barrier, len(devices))


def remote(src, dst, send, recv, number, device):
    return pltpu.make_async_remote_copy(
        src_ref=src,
        dst_ref=dst,
        send_sem=send.at[number],
        recv_sem=recv.at[number],
        device_id=device,
        device_id_type=MESH,
    )


def pack_edges(src, base, dst):
    @pl.loop(0, dst.shape[0])
    def _(group):
        total = None
        for e in range(PER):
            x = src[base + group * PER + e]
            lane = lane_index(x.shape)
            x = jnp.where((lane < HALO) | (lane >= LANES - HALO), x, 0.0)
            x = roll(x, (HALO + SLOT * e) % LANES)
            total = x if total is None else total + x
        dst[group] = total


def pack_rows(src, base, low, high):
    @pl.loop(0, low.shape[0])
    def _(block):
        for i in range(QUAD):
            at = base + block * QUAD + i
            to = pl.ds(HALO * i, HALO)
            low[block, to] = src[at, 0:HALO].astype(jnp.float32)
            high[block, to] = src[at, 16 - HALO : 16].astype(jnp.float32)


def unpack_rows(src, base, left, right, dst):
    @pl.loop(0, left.shape[0])
    def _(block):
        for i in range(QUAD):
            at = block * QUAD + i
            of = pl.ds(HALO * i, HALO)
            dst[at, 8 - HALO : 8] = left[block, of]
            dst[at, 8:24] = src[base + at]
            dst[at, 24 : 24 + HALO] = right[block, of]


def store_weights(dst, rows, offset, frac):
    rest = 1.0 - frac
    before = None
    for pos, total in enumerate(SHIFTS):
        here = offset == total
        second = 0.0 if before is None else jnp.where(before, frac, 0.0)
        dst[pos, rows] = jnp.where(here, rest, second)
        before = here


def factor(dims, coup, ratio, inverse):
    fields, levels = dims
    previous = [None] * fields
    for k in range(levels):
        for f in range(fields):
            at, c = f * levels + k, f * (levels - 1) + k
            denom = 1.0
            if k > 0:
                below = coup[c - 1]
                denom = denom + below
            if k < levels - 1:
                above = coup[c]
                denom = denom + above
            if k > 0:
                denom = denom - below * previous[f]
            inv = 1.0 / denom
            inverse[at] = inv
            if k < levels - 1:
                previous[f] = above * inv
                ratio[at] = previous[f]


def advect(dims, first_field, band, bands, wide, edges, lonw, latw, coup, inverse, shifted, prime):
    fields, levels = dims
    has_lower = band > 0
    has_upper = band < bands - 1

    @pl.loop(0, PAIR)
    def _(member):
        @pl.loop(0, levels)
        def _(k):
            local = member * levels + k
            f = first_field + member
            at = f * levels + k
            main = wide[local]
            group, slot = local // PER, local % PER
            shift = lax.rem(2 * LANES - HALO - SLOT * slot, LANES)
            lane = lane_index(main.shape)
            lower = jnp.where(has_lower, roll(edges[0, group], shift), 0.0)
            upper = jnp.where(has_upper, roll(edges[1, group], shift), 0.0)
            edge = jnp.where(lane < LANES // 2, upper, lower)
            for pos, total in enumerate(SHIFTS):
                t = -total
                if t == 0:
                    shifted[pos] = main
                    continue
                inside = (lane >= LANES + t) if t < 0 else (lane < t)
                shifted[pos] = roll(jnp.where(inside, edge, main), (-t) % LANES)
            c = f * (levels - 1) + k
            first = k == 0
            for half in range(2):
                rows = pl.ds(8 * half, 8)
                inner_rows = pl.ds(8 + 8 * half, 8)
                lat = [latw[k, pos, inner_rows] for pos in range(len(SHIFTS))]
                adv = None
                for lon_pos, lon_total in enumerate(SHIFTS):
                    inner = None
                    start = 8 + 8 * half - lon_total
                    for pos in range(len(SHIFTS)):
                        term = lat[pos] * shifted[pos, pl.ds(start, 8)]
                        inner = term if inner is None else inner + term
                    term = lonw[k, lon_pos, inner_rows] * inner
                    adv = term if adv is None else adv + term
                below = jnp.where(first, 0.0, coup[jnp.where(first, c, c - 1), rows])
                before = jnp.where(first, 0.0, prime[jnp.where(first, at, at - 1), rows])
                prime[at, rows] = (adv + below * before) * inverse[at, rows]


def solve(dims, first_field, prime, ratio, inverse, coup, dep, weight, tl, z):
    fields, levels = dims
    members = range(first_field, first_field + PAIR)
    x = {}
    for k in range(levels - 1, -1, -1):
        for f in members:
            at = f * levels + k
            x[f] = prime[at] if k == levels - 1 else prime[at] + ratio[at] * x[f]
            tl[at] = x[f]
    for k in range(levels):
        for f in members:
            at = f * levels + k
            forcing = weight[at] * (tl[at] - dep[at])
            if k > 0:
                forcing = forcing + coup[f * (levels - 1) + k - 1] * x[f]
            x[f] = forcing * inverse[at]
            prime[at] = x[f]
    for k in range(levels - 1, -1, -1):
        for f in members:
            at = f * levels + k
            x[f] = prime[at] if k == levels - 1 else prime[at] + ratio[at] * x[f]
            z[at] = x[f]


def collect(dims, first_field, wide, lonw, latw, inc, grad, spill):
    fields, levels = dims
    lane = lane_index((8, LANES))

    @pl.loop(0, levels)
    def _(k):
        for half in range(2):
            rows = pl.ds(8 * half, 8)
            sums = {}
            for lon_pos, lon_total in enumerate(SHIFTS):
                near = pl.ds(8 + 8 * half + lon_total, 8)
                scale = lonw[k, lon_pos, near]
                scaled = [scale * wide[f * levels + k, near] for f in range(PAIR)]
                for pos in range(len(SHIFTS)):
                    w = latw[k, pos, near]
                    for f in range(PAIR):
                        term = w * scaled[f]
                        sums[f, pos] = term if lon_pos == 0 else sums[f, pos] + term
            for f in range(PAIR):
                at = (first_field + f) * levels + k
                total, outside = inc[at, rows], jnp.zeros((8, LANES), jnp.float32)
                for pos, n in enumerate(SHIFTS):
                    if n == 0:
                        total = total + sums[f, pos]
                        continue
                    moved = roll(sums[f, pos], (-n) % LANES)
                    wraps = (lane >= LANES - n) if n > 0 else (lane < -n)
                    total = total + jnp.where(wraps, 0.0, moved)
                    outside = outside + jnp.where(wraps, moved, 0.0)
                grad[at, rows] = total
                spill[f * levels + k, rows] = outside


def finish(base, band, bands, edges, grad):
    has_lower = band > 0
    has_upper = band < bands - 1

    @pl.loop(0, edges.shape[1])
    def _(group):
        lower = jnp.where(has_lower, edges[0, group], 0.0)
        upper = jnp.where(has_upper, edges[1, group], 0.0)
        lane = lane_index(lower.shape)
        for e in range(PER):
            shift = (-HALO - SLOT * e) % LANES
            low = jnp.where(lane < HALO, roll(lower, shift), 0.0)
            high = jnp.where(lane >= LANES - HALO, roll(upper, shift), 0.0)
            at = base + group * PER + e
            grad[at] = grad[at] + (low + high)


def kernel(
    dims, sizes,
    inc_h, dep_h, weight_h, olon_h, olat_h, flon_h, flat_h, coup_h,
    tl_h, grad_h,
    inc, dep, weight, olon, olat, flon, flat, coup, tl, grad,
    low, high, from_left, from_right, edge_out, edge_in,
    g_low, g_high, g_left, g_right, z_low, z_high, z_left, z_right,
    back_out, back_in, spill, wide, shifted, lonw, latw, prime, ratio, inverse, z,
    load_sem, store_sem, send, recv,
):
    fields, levels = dims
    pairs = fields // PAIR
    per_pair = PAIR * levels
    at = neighbours(sizes)
    band, bands = lax.axis_index("lat"), sizes[0]
    numbers = iter(range(send.shape[0]))

    loads = [
        pltpu.make_async_copy(src, dst, load_sem.at[i])
        for i, (src, dst) in enumerate(
            [(inc_h, inc), (olon_h, olon), (olat_h, olat), (flon_h, flon), (flat_h, flat),
             (coup_h, coup), (dep_h, dep), (weight_h, weight)]
        )
    ]
    for load in loads:
        load.start()

    def launch(src, dst, device):
        copy = remote(src, dst, send, recv, next(numbers), device)
        copy.start()
        return copy

    greet([at(dy, dx) for dy in (-1, 0, 1) for dx in (-1, 0, 1) if (dy, dx) != (0, 0)])
    loads[0].wait()
    inward = []
    for pair in range(pairs):
        pack_rows(inc, pair * per_pair, low.at[pair], high.at[pair])
        copies = [
            launch(low.at[pair], from_right.at[pair], at(0, -1)),
            launch(high.at[pair], from_left.at[pair], at(0, 1)),
        ]
        packed = edge_out.at[pair]
        pack_edges(inc, pair * per_pair, packed)
        for dy in (-1, 1):
            side = edge_in.at[pair, 0 if dy == 1 else 1]
            copies.append(launch(packed, side.at[:, 8:24], at(dy, 0)))
            copies.append(launch(packed.at[:, 0:8], side.at[:, 24:32], at(dy, -1)))
            copies.append(launch(packed.at[:, 8:16], side.at[:, 0:8], at(dy, 1)))
        inward.append(copies)
    for load in loads[1:6]:
        load.wait()
    geometry = (olon, olat, flon, flat)
    blocks = levels // QUAD
    for i, own in enumerate(geometry):
        part = pl.ds(i * blocks, blocks)
        pack_rows(own, 0, g_low.at[part], g_high.at[part])
    around = [
        launch(g_low, g_right, at(0, -1)),
        launch(g_high, g_left, at(0, 1)),
    ]

    @pl.loop(0, levels)
    def _(k):
        store_weights(lonw.at[k], pl.ds(8, 16), olon[k], flon[k])
        store_weights(latw.at[k], pl.ds(8, 16), olat[k], flat[k])

    factor(dims, coup, ratio, inverse)
    for load in loads[6:]:
        load.wait()

    stores, across = [], []
    for pair in range(pairs):
        base = pair * per_pair
        for copy in inward[pair]:
            copy.wait()
        unpack_rows(inc, base, from_left.at[pair], from_right.at[pair], wide)
        advect(dims, pair * PAIR, band, bands, wide, edge_in.at[pair], lonw, latw, coup, inverse, shifted, prime)
        solve(dims, pair * PAIR, prime, ratio, inverse, coup, dep, weight, tl, z)
        pack_rows(z, base, z_low.at[pair], z_high.at[pair])
        across.append([
            launch(z_low.at[pair], z_right.at[pair], at(0, -1)),
            launch(z_high.at[pair], z_left.at[pair], at(0, 1)),
        ])
        part = pl.ds(base, per_pair)
        store = pltpu.make_async_copy(tl.at[part], tl_h.at[part], store_sem.at[pair])
        store.start()
        stores.append(store)

    for copy in around:
        copy.wait()

    @pl.loop(0, blocks)
    def _(block):
        for i in range(QUAD):
            k = block * QUAD + i
            of = pl.ds(HALO * i, HALO)
            for side, rows in ((g_left, pl.ds(8 - HALO, HALO)), (g_right, pl.ds(24, HALO))):
                parts = [side[number * blocks + block, of] for number in range(4)]
                store_weights(lonw.at[k], rows, parts[0], parts[2])
                store_weights(latw.at[k], rows, parts[1], parts[3])

    returned = []
    for pair in range(pairs):
        base = pair * per_pair
        for copy in across[pair]:
            copy.wait()
        unpack_rows(z, base, z_left.at[pair], z_right.at[pair], wide)
        collect(dims, pair * PAIR, wide, lonw, latw, inc, grad, spill)
        pack_edges(spill, 0, back_out.at[pair])
        returned.append([
            launch(back_out.at[pair], back_in.at[pair, 1], at(-1, 0)),
            launch(back_out.at[pair], back_in.at[pair, 0], at(1, 0)),
        ])
    for pair in range(pairs):
        base = pair * per_pair
        for copy in returned[pair]:
            copy.wait()
        finish(base, band, bands, back_in.at[pair], grad)
        part = pl.ds(base, per_pair)
        store = pltpu.make_async_copy(grad.at[part], grad_h.at[part], store_sem.at[pairs + pair])
        store.start()
        stores.append(store)
    for store in stores:
        store.wait()


def shards(sizes, increment, obs_dep, obs_weight, dep_lon, dep_lat, frac_lon, frac_lat, coupling):
    fields, levels, rows, cols = increment.shape
    count = fields * levels
    pairs = fields // PAIR
    groups = PAIR * levels // PER
    quads = PAIR * levels // QUAD
    dims = (fields, levels)

    def vmem(*s, dtype=jnp.float32):
        return pltpu.VMEM(s, dtype)

    def flat3(x):
        return x.reshape(-1, rows, cols)

    whole = jax.ShapeDtypeStruct((count, rows, cols), jnp.float32)
    field = vmem(count, rows, cols)
    level = vmem(levels, rows, cols)
    index = vmem(levels, rows, cols, dtype=jnp.int32)
    halo = vmem(pairs, quads, QUAD * HALO, cols)
    g_halo = vmem(4 * levels // QUAD, QUAD * HALO, cols)
    weights = vmem(levels, len(SHIFTS), 32, cols)
    copies = pairs * 12 + 2
    tl, grad = pl.pallas_call(
        functools.partial(kernel, dims, sizes),
        out_shape=(whole, whole),
        in_specs=[ANY] * 8,
        out_specs=(ANY, ANY),
        scratch_shapes=[
            field, field, field, index, index, level, level,
            vmem(fields * (levels - 1), rows, cols), field, field,
            halo, halo, halo, halo,
            vmem(pairs, groups, rows, cols), vmem(pairs, 2, groups, 32, cols),
            g_halo, g_halo, g_halo, g_halo, halo, halo, halo, halo,
            vmem(pairs, groups, rows, cols), vmem(pairs, 2, groups, rows, cols),
            vmem(PAIR * levels, rows, cols), vmem(PAIR * levels, 32, cols),
            vmem(len(SHIFTS), 32, cols), weights, weights, field, field, field, field,
            pltpu.SemaphoreType.DMA((8,)),
            pltpu.SemaphoreType.DMA((2 * pairs,)),
            pltpu.SemaphoreType.DMA((copies,)),
            pltpu.SemaphoreType.DMA((copies,)),
        ],
        compiler_params=pltpu.CompilerParams(
            collective_id=0, has_side_effects=True, vmem_limit_bytes=LIMIT
        ),
    )(
        flat3(increment), flat3(obs_dep), flat3(obs_weight), dep_lon, dep_lat, frac_lon, frac_lat,
        flat3(coupling),
    )
    return tl.reshape(increment.shape), grad.reshape(increment.shape)


def solution(mesh):
    sizes = (mesh.shape["lat"], mesh.shape["lon"])
    wide = P(None, None, "lon", "lat")
    level = P(None, "lon", "lat")
    return jax.shard_map(
        functools.partial(shards, sizes),
        mesh=mesh,
        in_specs=(wide, wide, wide, level, level, level, level, wide),
        out_specs=(wide, wide),
        check_vma=False,
    )
```

time: 86.8 us -> 53.3 us (0.61)
  Pallas kernels: 79.3 us -> 49.6 us
  starting transfers between devices: 4.54 us -> 0 us
  local copies, waits for them, and re-layouts: 0.94 us -> 2.89 us
  other arithmetic: 1.11 us -> 0 us
    pallas_call x6 -> x1, Pallas kernels: 79.3 us -> 49.6 us  [shards(): pl.pallas_call(functools.partial(kernel, dims, sizes), out_shape=(whole,...]
    ppermute x2 -> x0, starting transfers between devices: 4.54 us -> none  [the longest x1 4.54 us: shards(): lax.ppermute(geometry[:, :, 0:8], 'lon', [((i + 1) % n, i) for i in range...]
    unnamed x8 -> x4, local copies, waits for them, and re-layouts: 0.9 us -> 2.89 us
    another operation x2 -> x0, other arithmetic: 1.11 us -> none  [shards(): jnp.stack([dep_lon.astype(f32), dep_lat.astype(f32), frac_lon, frac_lat])]
  transfers between devices with their start and end apart: 2 -> 0, of which waited for: 0 -> 0; matrix products, arithmetic and copies ran while one was open for 0% -> 0% of each run, Pallas kernels for 64% -> 0%
where the time goes in v2:
time: 53.3 us; the launch traced here: 53.2 us
  Pallas kernels  49.6 us (93%)
  local copies, waits for them, and re-layouts  2.89 us (5%)
  between operations  0.65 us (1%)
    pallas_call x1, Pallas kernels, shards(): pl.pallas_call(functools.partial(kernel, dims, sizes), out_shape=(whole,...  49.6 us
    unnamed x4, local copies, waits for them, and re-layouts  2.89 us

profile of v2, /device:TPU:0, one launch (start us, length us, event | category | flops | bytes accessed | tf_op | source)
XLA Modules:
  0.0 53.2 jit_solution(14679222494402290407)
XLA Ops:
  0.6 49.6 %shard_map.95 = (f32[80,16,128]{2,1,0:T(8,128)}, f32[80,16,128]{2,1,0:T(8,128)}) custom-call(f32[80,16,128]{2,1,0:T(8,128)} %bitcast.8, f32[80,16,128]{2,1,0:T(8,128)} %bitcast.9, f32[80,16,128]{2,1,0:T(8,128)} %bitcast.10, s32[20,16,128]{2,1,0:T(8,128)} %olon_h.1, s32[20,16,128]{2,1,0:T(8,128)} %olat_h.1, f32[20,16,128]{2,1,0:T(8,128)} %flon_h.1, ...), custom_call_target="tpu_custom_call" | custom-call | tf_op jit(solution)/shard_map/pallas_call | solution.py:394
  50.3 0.0 copy-start
  50.3 2.0 %copy.12 = f32[4,20,16,128]{3,2,1,0:T(8,128)} copy(f32[4,20,16,128]{3,2,1,0:T(8,128)} %bitcast.7) | data formatting | bytes 1310720
  52.3 0.0 copy-done
  52.3 0.8 %copy.13 = f32[4,20,16,128]{3,2,1,0:T(8,128)} copy(f32[4,20,16,128]{3,2,1,0:T(8,128)S(1)} %bitcast.6) | data formatting | bytes 1310720
Async XLA Ops:
  50.3 2.1 %copy-start = (f32[80,16,128]{2,1,0:T(8,128)S(1)}, f32[80,16,128]{2,1,0:T(8,128)}, u32[]{:S(2)}) copy-start(f32[80,16,128]{2,1,0:T(8,128)} %get-tuple-element.5) | copy-start | bytes 1966084

commit v3 on v2

--- a/solution.py
+++ b/solution.py
@@ -128,45 +128,47 @@
     has_lower = band > 0
     has_upper = band < bands - 1
 
-    @pl.loop(0, PAIR)
-    def _(member):
-        @pl.loop(0, levels)
-        def _(k):
+    @pl.loop(0, levels)
+    def _(k):
+        lane = lane_index(wide.shape[1:])
+        for member in range(PAIR):
             local = member * levels + k
-            f = first_field + member
-            at = f * levels + k
             main = wide[local]
             group, slot = local // PER, local % PER
             shift = lax.rem(2 * LANES - HALO - SLOT * slot, LANES)
-            lane = lane_index(main.shape)
             lower = jnp.where(has_lower, roll(edges[0, group], shift), 0.0)
             upper = jnp.where(has_upper, roll(edges[1, group], shift), 0.0)
             edge = jnp.where(lane < LANES // 2, upper, lower)
             for pos, total in enumerate(SHIFTS):
                 t = -total
                 if t == 0:
-                    shifted[pos] = main
+                    shifted[member, pos] = main
                     continue
                 inside = (lane >= LANES + t) if t < 0 else (lane < t)
-                shifted[pos] = roll(jnp.where(inside, edge, main), (-t) % LANES)
-            c = f * (levels - 1) + k
-            first = k == 0
-            for half in range(2):
-                rows = pl.ds(8 * half, 8)
-                inner_rows = pl.ds(8 + 8 * half, 8)
-                lat = [latw[k, pos, inner_rows] for pos in range(len(SHIFTS))]
-                adv = None
-                for lon_pos, lon_total in enumerate(SHIFTS):
-                    inner = None
-                    start = 8 + 8 * half - lon_total
-                    for pos in range(len(SHIFTS)):
-                        term = lat[pos] * shifted[pos, pl.ds(start, 8)]
-                        inner = term if inner is None else inner + term
-                    term = lonw[k, lon_pos, inner_rows] * inner
-                    adv = term if adv is None else adv + term
+                shifted[member, pos] = roll(jnp.where(inside, edge, main), (-t) % LANES)
+        first = k == 0
+        for half in range(2):
+            rows = pl.ds(8 * half, 8)
+            inner_rows = pl.ds(8 + 8 * half, 8)
+            advected = [None] * PAIR
+            for lon_pos, lon_total in enumerate(SHIFTS):
+                near = pl.ds(8 + 8 * half - lon_total, 8)
+                inner = [None] * PAIR
+                for pos in range(len(SHIFTS)):
+                    w = latw[k, pos, inner_rows]
+                    for member in range(PAIR):
+                        term = w * shifted[member, pos, near]
+                        inner[member] = term if pos == 0 else inner[member] + term
+                w = lonw[k, lon_pos, inner_rows]
+                for member in range(PAIR):
+                    term = w * inner[member]
+                    advected[member] = term if lon_pos == 0 else advected[member] + term
+            for member in range(PAIR):
+                f = first_field + member
+                at, c = f * levels + k, f * (levels - 1) + k
                 below = jnp.where(first, 0.0, coup[jnp.where(first, c, c - 1), rows])
                 before = jnp.where(first, 0.0, prime[jnp.where(first, at, at - 1), rows])
-                prime[at, rows] = (adv + below * before) * inverse[at, rows]
+                prime[at, rows] = (advected[member] + below * before) * inverse[at, rows]
 
 
 def solve(dims, first_field, prime, ratio, inverse, coup, dep, weight, tl, z):
@@ -279,18 +281,17 @@
     loads[0].wait()
     inward = []
     for pair in range(pairs):
-        pack_rows(inc, pair * per_pair, low.at[pair], high.at[pair])
-        copies = [
-            launch(low.at[pair], from_right.at[pair], at(0, -1)),
-            launch(high.at[pair], from_left.at[pair], at(0, 1)),
-        ]
+        copies = []
         packed = edge_out.at[pair]
         pack_edges(inc, pair * per_pair, packed)
         for dy in (-1, 1):
             side = edge_in.at[pair, 0 if dy == 1 else 1]
-            copies.append(launch(packed, side.at[:, 8:24], at(dy, 0)))
             copies.append(launch(packed.at[:, 0:8], side.at[:, 24:32], at(dy, -1)))
             copies.append(launch(packed.at[:, 8:16], side.at[:, 0:8], at(dy, 1)))
+            copies.append(launch(packed, side.at[:, 8:24], at(dy, 0)))
+        pack_rows(inc, pair * per_pair, low.at[pair], high.at[pair])
+        copies.append(launch(low.at[pair], from_right.at[pair], at(0, -1)))
+        copies.append(launch(high.at[pair], from_left.at[pair], at(0, 1)))
         inward.append(copies)
     for load in loads[1:6]:
         load.wait()
@@ -404,7 +405,7 @@
             g_halo, g_halo, g_halo, g_halo, halo, halo, halo, halo,
             vmem(pairs, groups, rows, cols), vmem(pairs, 2, groups, rows, cols),
             vmem(PAIR * levels, rows, cols), vmem(PAIR * levels, 32, cols),
-            vmem(len(SHIFTS), 32, cols), weights, weights, field, field, field, field,
+            vmem(PAIR, len(SHIFTS), 32, cols), weights, weights, field, field, field, field,
             pltpu.SemaphoreType.DMA((8,)),
             pltpu.SemaphoreType.DMA((2 * pairs,)),
             pltpu.SemaphoreType.DMA((copies,)),

time: 53.3 us -> 48.5 us (0.910)
  Pallas kernels: 49.6 us -> 44.8 us
    pallas_call x1, Pallas kernels: 49.6 us -> 44.8 us  [shards(): pl.pallas_call(functools.partial(kernel, dims, sizes), out_shape=(whole,...]
where the time goes in v3:
time: 48.5 us; the launch traced here: 48.3 us
  Pallas kernels  44.8 us (92%)
  local copies, waits for them, and re-layouts  2.89 us (6%)
  between operations  0.65 us (1%)
    pallas_call x1, Pallas kernels, shards(): pl.pallas_call(functools.partial(kernel, dims, sizes), out_shape=(whole,...  44.8 us
    unnamed x4, local copies, waits for them, and re-layouts  2.89 us

profile of v3, /device:TPU:0, one launch (start us, length us, event | category | flops | bytes accessed | tf_op | source)
XLA Modules:
  0.0 48.3 jit_solution(6652619114923447755)
XLA Ops:
  0.6 44.8 %shard_map.95 = (f32[80,16,128]{2,1,0:T(8,128)}, f32[80,16,128]{2,1,0:T(8,128)}) custom-call(f32[80,16,128]{2,1,0:T(8,128)} %bitcast.8, f32[80,16,128]{2,1,0:T(8,128)} %bitcast.9, f32[80,16,128]{2,1,0:T(8,128)} %bitcast.10, s32[20,16,128]{2,1,0:T(8,128)} %olon_h.1, s32[20,16,128]{2,1,0:T(8,128)} %olat_h.1, f32[20,16,128]{2,1,0:T(8,128)} %flon_h.1, ...), custom_call_target="tpu_custom_call" | custom-call | tf_op jit(solution)/shard_map/pallas_call | solution.py:395
  45.4 0.0 copy-start
  45.4 2.0 %copy.12 = f32[4,20,16,128]{3,2,1,0:T(8,128)} copy(f32[4,20,16,128]{3,2,1,0:T(8,128)} %bitcast.7) | data formatting | bytes 1310720
  47.5 0.0 copy-done
  47.5 0.8 %copy.13 = f32[4,20,16,128]{3,2,1,0:T(8,128)} copy(f32[4,20,16,128]{3,2,1,0:T(8,128)S(1)} %bitcast.6) | data formatting | bytes 1310720
Async XLA Ops:
  45.4 2.1 %copy-start = (f32[80,16,128]{2,1,0:T(8,128)S(1)}, f32[80,16,128]{2,1,0:T(8,128)}, u32[]{:S(2)}) copy-start(f32[80,16,128]{2,1,0:T(8,128)} %get-tuple-element.5) | copy-start | bytes 1966084

commit v4 on v3

--- a/solution.py
+++ b/solution.py
@@ -147,28 +147,31 @@
                 inside = (lane >= LANES + t) if t < 0 else (lane < t)
                 shifted[member, pos] = roll(jnp.where(inside, edge, main), (-t) % LANES)
         first = k == 0
+        advected = {}
+        for start in range(8 - HALO, 16 + HALO):
+            users = [(half, 8 + 8 * half - start) for half in range(2) if 8 + 8 * half - start in SHIFTS]
+            inner = {}
+            for pos in range(len(SHIFTS)):
+                sources = [shifted[member, pos, pl.ds(start, 8)] for member in range(PAIR)]
+                for half, _ in users:
+                    w = latw[k, pos, pl.ds(8 + 8 * half, 8)]
+                    for member in range(PAIR):
+                        term = w * sources[member]
+                        inner[half, member] = term if pos == 0 else inner[half, member] + term
+            for half, lon_total in users:
+                w = lonw[k, lon_total + HALO - 1, pl.ds(8 + 8 * half, 8)]
+                for member in range(PAIR):
+                    term = w * inner[half, member]
+                    old = advected.get((half, member))
+                    advected[half, member] = term if old is None else old + term
         for half in range(2):
             rows = pl.ds(8 * half, 8)
-            inner_rows = pl.ds(8 + 8 * half, 8)
-            advected = [None] * PAIR
-            for lon_pos, lon_total in enumerate(SHIFTS):
-                near = pl.ds(8 + 8 * half - lon_total, 8)
-                inner = [None] * PAIR
-                for pos in range(len(SHIFTS)):
-                    w = latw[k, pos, inner_rows]
-                    for member in range(PAIR):
-                        term = w * shifted[member, pos, near]
-                        inner[member] = term if pos == 0 else inner[member] + term
-                w = lonw[k, lon_pos, inner_rows]
-                for member in range(PAIR):
-                    term = w * inner[member]
-                    advected[member] = term if lon_pos == 0 else advected[member] + term
             for member in range(PAIR):
                 f = first_field + member
                 at, c = f * levels + k, f * (levels - 1) + k
                 below = jnp.where(first, 0.0, coup[jnp.where(first, c, c - 1), rows])
                 before = jnp.where(first, 0.0, prime[jnp.where(first, at, at - 1), rows])
-                prime[at, rows] = (advected[member] + below * before) * inverse[at, rows]
+                prime[at, rows] = (advected[half, member] + below * before) * inverse[at, rows]
 
 
 def solve(dims, first_field, prime, ratio, inverse, coup, dep, weight, tl, z):

time: 48.5 us -> 48.9 us (level)
  no operation moved by 1% of the time
where the time goes in v4:
time: 48.9 us; the launch traced here: 48.7 us
  Pallas kernels  45.2 us (92%)
  local copies, waits for them, and re-layouts  2.89 us (6%)
  between operations  0.65 us (1%)
    pallas_call x1, Pallas kernels, shards(): pl.pallas_call(functools.partial(kernel, dims, sizes), out_shape=(whole,...  45.2 us
    unnamed x4, local copies, waits for them, and re-layouts  2.89 us

profile of v4, /device:TPU:0, one launch (start us, length us, event | category | flops | bytes accessed | tf_op | source)
XLA Modules:
  0.0 48.7 jit_solution(16040056837106095898)
XLA Ops:
  0.6 45.2 %shard_map.95 = (f32[80,16,128]{2,1,0:T(8,128)}, f32[80,16,128]{2,1,0:T(8,128)}) custom-call(f32[80,16,128]{2,1,0:T(8,128)} %bitcast.8, f32[80,16,128]{2,1,0:T(8,128)} %bitcast.9, f32[80,16,128]{2,1,0:T(8,128)} %bitcast.10, s32[20,16,128]{2,1,0:T(8,128)} %olon_h.1, s32[20,16,128]{2,1,0:T(8,128)} %olat_h.1, f32[20,16,128]{2,1,0:T(8,128)} %flon_h.1, ...), custom_call_target="tpu_custom_call" | custom-call | tf_op jit(solution)/shard_map/pallas_call | solution.py:398
  45.9 0.0 copy-start
  45.9 2.0 %copy.12 = f32[4,20,16,128]{3,2,1,0:T(8,128)} copy(f32[4,20,16,128]{3,2,1,0:T(8,128)} %bitcast.7) | data formatting | bytes 1310720
  47.9 0.0 copy-done
  47.9 0.8 %copy.13 = f32[4,20,16,128]{3,2,1,0:T(8,128)} copy(f32[4,20,16,128]{3,2,1,0:T(8,128)S(1)} %bitcast.6) | data formatting | bytes 1310720
Async XLA Ops:
  45.9 2.1 %copy-start = (f32[80,16,128]{2,1,0:T(8,128)S(1)}, f32[80,16,128]{2,1,0:T(8,128)}, u32[]{:S(2)}) copy-start(f32[80,16,128]{2,1,0:T(8,128)} %get-tuple-element.5) | copy-start | bytes 1966084
